TPU v7x, 512 devices: a whole 4x4x16 slice. The times are simulated.
512 devices in a mesh: rep: 4 (over y), shard: 32 (over z, core), tp: 4 (over x).
Axes of the slice: x: 4, y: 4, z: 16, core: 2. Of those that a mesh axis runs over, the one named last changes fastest.
Arguments:
- qkv_grad: bfloat16 [4, 1024, 3072], P('rep', 'shard', 'tp'), may hold values from -100 to 100
- qkv_error: float32 [4, 1024, 3072], P('rep', 'shard', 'tp'), may hold values from -4 to 4
- qkv_basis: float32 [3072, 32], P('tp'), may hold values from -6 to 6
- qkv_weight: float32 [32, 4, 8, 3072], P('shard', 'rep', None, 'tp'), may hold values from -0.75 to 0.75
- qkv_moment: float32 [32, 4, 8, 3072], P('shard', 'rep', None, 'tp'), may hold values from -0.75 to 0.75
- gu_grad: bfloat16 [4, 1024, 8192], P('rep', 'shard', 'tp'), may hold values from -100 to 100
- gu_error: float32 [4, 1024, 8192], P('rep', 'shard', 'tp'), may hold values from -4 to 4
- gu_basis: float32 [8192, 32], P('tp'), may hold values from -6 to 6
- gu_weight: float32 [32, 4, 8, 8192], P('shard', 'rep', None, 'tp'), may hold values from -0.75 to 0.75
- gu_moment: float32 [32, 4, 8, 8192], P('shard', 'rep', None, 'tp'), may hold values from -0.75 to 0.75
- down_grad: bfloat16 [4, 4096, 1024], P('rep', 'shard', 'tp'), may hold values from -100 to 100
- down_error: float32 [4, 4096, 1024], P('rep', 'shard', 'tp'), may hold values from -4 to 4
- down_basis: float32 [1024, 32], P('tp'), may hold values from -6 to 6
- down_weight: float32 [32, 4, 32, 1024], P('shard', 'rep', None, 'tp'), may hold values from -0.75 to 0.75
- down_moment: float32 [32, 4, 32, 1024], P('shard', 'rep', None, 'tp'), may hold values from -0.75 to 0.75
- vec_grad: bfloat16 [4, 11264], P('rep', ('shard', 'tp')), may hold values from -6 to 6
- vec_weight: float32 [11264], P(('shard', 'tp')), may hold values from 0.5 to 1.5
- vec_moment: float32 [11264], P(('shard', 'tp')), may hold values from -6 to 6
- emb_ids: int32 [4, 4096], P('rep', 'shard'), may hold values from 0 to 31999
- emb_grad: bfloat16 [4, 4096, 1024], P('rep', 'shard', 'tp'), may hold values from -6 to 6
- emb_weight: float32 [32, 4, 250, 1024], P('shard', 'rep', None, 'tp'), may hold values from -0.75 to 0.75
- emb_moment: float32 [32, 4, 250, 1024], P('shard', 'rep', None, 'tp'), may hold values from -6 to 6
Outputs:
- qkv_new: float32 [1024, 3072], P('shard', 'tp')
- qkv_error_new: float32 [4, 1024, 3072], P('rep', 'shard', 'tp')
- qkv_moment_new: float32 [32, 4, 8, 3072], P('shard', 'rep', None, 'tp')
- gu_new: float32 [1024, 8192], P('shard', 'tp')
- gu_error_new: float32 [4, 1024, 8192], P('rep', 'shard', 'tp')
- gu_moment_new: float32 [32, 4, 8, 8192], P('shard', 'rep', None, 'tp')
- down_new: float32 [4096, 1024], P('shard', 'tp')
- down_error_new: float32 [4, 4096, 1024], P('rep', 'shard', 'tp')
- down_moment_new: float32 [32, 4, 32, 1024], P('shard', 'rep', None, 'tp')
- vec_new: float32 [11264], P(('shard', 'tp'))
- vec_moment_new: float32 [11264], P(('shard', 'tp'))
- emb_new: float32 [32000, 1024], P('shard', 'tp')
- emb_moment_new: float32 [32, 4, 250, 1024], P('shard', 'rep', None, 'tp')
All inputs are finite; a program needn't handle non-finite values.
Results may differ from a plain program's by a relative error of at most 0.0004.
Values may be sent and summed in bfloat16 or wider, within the bound.
A program may use at most 64 MiB of HBM per device.

v0:
```python
import jax
import jax.numpy as jnp
from jax import lax
from jax.sharding import PartitionSpec as P

ROUNDS = 2
momentum_decay = 0.9
step_size = 0.05


def solve_right(lower_factor, values):
    return jax.scipy.linalg.solve_triangular(lower_factor, values.T, lower=True).T


def dot_high(left_side, right_side):
    return jnp.dot(left_side, right_side, precision=lax.Precision.HIGHEST)


def add_rows(running, row_ids, row_values, row_start, block_rows):

    def one_block(partial_sum, block_ids, block_values):
        local_ids = block_ids - row_start
        one_hot = (
            local_ids[None, :]
            == lax.broadcasted_iota(jnp.int32, (block_rows, block_ids.shape[0]), 0)
        ).astype(jnp.bfloat16)
        return partial_sum + jnp.dot(one_hot, block_values, preferred_element_type=jnp.float32)

    count = row_ids.shape[0]
    width = 512
    split_ids = row_ids.reshape(count // width, width)
    split_values = row_values.reshape(count // width, width, row_values.shape[-1])

    def scan_step(partial_sum, inputs):
        return (one_block(partial_sum, inputs[0], inputs[1]), None)

    return lax.scan(scan_step, running, (split_ids, split_values))[0]


def on_device(
    qkv_grad,
    qkv_error,
    qkv_basis,
    qkv_weight,
    qkv_moment,
    gu_grad,
    gu_error,
    gu_basis,
    gu_weight,
    gu_moment,
    down_grad,
    down_error,
    down_basis,
    down_weight,
    down_moment,
    vec_grad,
    vec_weight,
    vec_moment,
    emb_ids,
    emb_grad,
    emb_weight,
    emb_moment,
):
    rep_count = lax.axis_size("rep")
    rep_index = lax.axis_index("rep")
    shard_index = lax.axis_index("shard")
    fulls = [
        qkv_grad[0].astype(jnp.float32) + qkv_error[0],
        gu_grad[0].astype(jnp.float32) + gu_error[0],
        down_grad[0].astype(jnp.float32) + down_error[0],
    ]
    rights = [qkv_basis, gu_basis, down_basis]
    lefts = rights
    for round_index in range(ROUNDS):
        parts = [
            dot_high(full_grad, right_factor) for full_grad, right_factor in zip(fulls, rights)
        ]
        lefts = [lax.psum(left_part, ("rep", "tp")) for left_part in parts]
        grams = [dot_high(left_factor.T, left_factor) for left_factor in lefts]
        summed = lax.psum((grams[0], grams[1], grams[2]), "shard")
        lowers = [jnp.linalg.cholesky(summed[index]) for index in range(3)]
        lefts = [solve_right(lowers[index], lefts[index]) for index in range(3)]
        raw_rights = [
            dot_high(full_grad.T, left_factor) for full_grad, left_factor in zip(fulls, lefts)
        ]
        rights = list(lax.psum((raw_rights[0], raw_rights[1], raw_rights[2]), ("rep", "shard")))
    errors_new = []
    moments_new = []
    flats_new = []
    for index, (weight, moment) in enumerate(
        ((qkv_weight, qkv_moment), (gu_weight, gu_moment), (down_weight, down_moment))
    ):
        approx = dot_high(lefts[index], rights[index].T) / rep_count
        errors_new.append((fulls[index] - approx)[None])
        local_rows = weight.shape[2]
        own_rows = lax.dynamic_slice_in_dim(approx, rep_index * local_rows, local_rows, 0)
        moment_new = momentum_decay * moment[0, 0] + own_rows
        moments_new.append(moment_new[None, None])
        flats_new.append((weight[0, 0] - step_size * moment_new)[None, None])
    vec_mean = lax.psum(vec_grad[0].astype(jnp.float32), "rep") / rep_count
    vec_moment_new = momentum_decay * vec_moment + vec_mean
    vec_new = vec_weight - step_size * vec_moment_new
    block_rows = emb_weight.shape[2]
    row_width = emb_grad.shape[2]
    row_start = (shard_index * rep_count + rep_index) * block_rows
    initial = jnp.zeros((block_rows, row_width), jnp.float32)
    pieces = (
        lax.all_gather(emb_ids, ("rep", "shard"), axis=1, tiled=True),
        lax.all_gather(emb_grad, ("rep", "shard"), axis=1, tiled=True),
    )
    row_ids = pieces[0].reshape(-1)
    row_values = pieces[1].reshape(-1, pieces[1].shape[-1])
    emb_sum = add_rows(initial, row_ids, row_values, row_start, block_rows) / rep_count
    emb_moment_new = momentum_decay * emb_moment[0, 0] + emb_sum
    emb_flat_new = (emb_weight[0, 0] - step_size * emb_moment_new)[None, None]
    gathered = (
        lax.all_gather(flats_new[0], "rep", axis=1, tiled=True),
        lax.all_gather(flats_new[1], "rep", axis=1, tiled=True),
        lax.all_gather(flats_new[2], "rep", axis=1, tiled=True),
        lax.all_gather(emb_flat_new, "rep", axis=1, tiled=True),
    )
    plains = [whole.reshape(whole.shape[1] * whole.shape[2], whole.shape[3]) for whole in gathered]
    return (
        plains[0],
        errors_new[0],
        moments_new[0],
        plains[1],
        errors_new[1],
        moments_new[1],
        plains[2],
        errors_new[2],
        moments_new[2],
        vec_new,
        vec_moment_new,
        plains[3],
        emb_moment_new[None, None],
    )


def solution(mesh):
    return jax.shard_map(
        on_device,
        mesh=mesh,
        in_specs=(
            P("rep", "shard", "tp"),
            P("rep", "shard", "tp"),
            P("tp", None),
            P("shard", "rep", None, "tp"),
            P("shard", "rep", None, "tp"),
            P("rep", "shard", "tp"),
            P("rep", "shard", "tp"),
            P("tp", None),
            P("shard", "rep", None, "tp"),
            P("shard", "rep", None, "tp"),
            P("rep", "shard", "tp"),
            P("rep", "shard", "tp"),
            P("tp", None),
            P("shard", "rep", None, "tp"),
            P("shard", "rep", None, "tp"),
            P("rep", ("shard", "tp")),
            P(("shard", "tp")),
            P(("shard", "tp")),
            P("rep", "shard"),
            P("rep", "shard", "tp"),
            P("shard", "rep", None, "tp"),
            P("shard", "rep", None, "tp"),
        ),
        out_specs=(
            P("shard", "tp"),
            P("rep", "shard", "tp"),
            P("shard", "rep", None, "tp"),
            P("shard", "tp"),
            P("rep", "shard", "tp"),
            P("shard", "rep", None, "tp"),
            P("shard", "tp"),
            P("rep", "shard", "tp"),
            P("shard", "rep", None, "tp"),
            P(("shard", "tp")),
            P(("shard", "tp")),
            P("shard", "tp"),
            P("shard", "rep", None, "tp"),
        ),
        check_vma=False,
    )
```

profile of v0, /device:TPU:16, one launch (start us, length us, event | category | flops | bytes accessed | tf_op | source)
XLA Modules:
  0.0 1575.1 jit_solution(1362675693380436460)
XLA Ops:
  8.1 1.3 fusion.11
  9.4 1.2 fusion.20
  11.9 62.7 %all-reduce.5 = (f32[32,32]{1,0:T(8,128)S(1)}, f32[32,32]{1,0:T(8,128)S(1)}, f32[128,32]{0,1:T(8,128)S(1)}) all-reduce(f32[32,32]{1,0:T(8,128)S(1)} %fusion.29, f32[32,32]{1,0:T(8,128)S(1)} %fusion.11, f32[128,32]{0,1:T(8,128)S(1)} %fusion.20), channel_id=1, replica_groups=mesh['rep'=4,'shard'=32,'tp'=4] {'rep','tp'}, use_global_device_ids=true, to_apply=%region_0.0 | all-reduce | flops 6144 | bytes 49152 | tf_op jit(solution)/shard_map/psum | solution.py:78
  75.1 96.4 %all-reduce.3 = (f32[32,32]{0,1:T(8,128)S(1)}, f32[32,32]{0,1:T(8,128)S(1)}, f32[32,32]{0,1:T(8,128)S(1)}) all-reduce(f32[32,32]{0,1:T(8,128)S(1)} %fusion.68, f32[32,32]{0,1:T(8,128)S(1)} %fusion.70, f32[32,32]{0,1:T(8,128)S(1)} %fusion.72), channel_id=1, replica_groups=mesh['rep'=4,'shard'=32,'tp'=4] {'shard'}, use_global_device_ids=true, to_apply=%region_1.0 | all-reduce | flops 3072 | bytes 24576 | tf_op jit(solution)/shard_map/psum | solution.py:80
  171.7 2.9 cholesky.126
  176.0 2.4 custom-call.15
  178.7 2.1 fusion.9
  180.8 2.9 cholesky.104
  185.1 2.4 custom-call.13
  187.7 1.8 fusion.27
  189.6 2.9 cholesky.148
  193.8 2.4 custom-call.17
  197.6 418.9 %psum.147 = f32[256,32]{0,1:T(8,128)S(1)} all-reduce(f32[256,32]{0,1:T(8,128)S(1)} %fusion.18), channel_id=1, replica_groups=mesh['rep'=4,'shard'=32,'tp'=4] {'rep','shard'}, use_global_device_ids=true, to_apply=%region_16.0 | all-reduce | flops 8192 | bytes 65536 | tf_op jit(solution)/shard_map/psum | solution.py:86
  618.9 1.4 fusion.7
  620.3 141.7 %all-reduce.4 = (f32[32,32]{1,0:T(8,128)S(1)}, f32[32,32]{1,0:T(8,128)S(1)}, f32[128,32]{0,1:T(8,128)S(1)}) all-reduce(f32[32,32]{1,0:T(8,128)S(1)} %fusion.25, f32[32,32]{1,0:T(8,128)S(1)} %fusion.7, f32[128,32]{0,1:T(8,128)S(1)} %fusion.16), channel_id=1, replica_groups=mesh['rep'=4,'shard'=32,'tp'=4] {'rep','tp'}, use_global_device_ids=true, to_apply=%region_5.8 | all-reduce | flops 6144 | bytes 49152 | tf_op jit(solution)/shard_map/psum | solution.py:78
  762.6 90.1 %all-reduce.2 = (f32[32,32]{0,1:T(8,128)S(1)}, f32[32,32]{0,1:T(8,128)S(1)}, f32[32,32]{0,1:T(8,128)S(1)}) all-reduce(f32[32,32]{0,1:T(8,128)S(1)} %fusion.69, f32[32,32]{0,1:T(8,128)S(1)} %fusion.71, f32[32,32]{0,1:T(8,128)S(1)} %fusion.73), channel_id=1, replica_groups=mesh['rep'=4,'shard'=32,'tp'=4] {'shard'}, use_global_device_ids=true, to_apply=%region_6.9 | all-reduce | flops 3072 | bytes 24576 | tf_op jit(solution)/shard_map/psum | solution.py:80
  852.7 2.9 cholesky.137
  857.0 2.4 custom-call.16
  859.6 2.1 fusion.5
  861.8 2.9 cholesky.115
  866.0 2.4 custom-call.14
  868.7 1.8 fusion.23
  871.3 82.0 %all_gather.21 = s32[1,16384]{1,0:T(1,128)S(1)} all-gather(s32[1,128]{1,0:T(1,128)} %param.47), channel_id=1, replica_groups=mesh['rep'=4,'shard'=32,'tp'=4] {'rep','shard'}, dimensions={1}, use_global_device_ids=true | all-gather | bytes 66048 | tf_op jit(solution)/shard_map/all_gather | solution.py:108
  955.2 9.1 psum.151
  965.7 2.9 cholesky.159
  969.9 2.4 custom-call.18
  973.7 415.1 %psum.150 = f32[256,32]{0,1:T(8,128)S(1)} all-reduce(f32[256,32]{0,1:T(8,128)S(1)} %fusion.14), channel_id=1, replica_groups=mesh['rep'=4,'shard'=32,'tp'=4] {'rep','shard'}, use_global_device_ids=true, to_apply=%region_19.23 | all-reduce | flops 8192 | bytes 65536 | tf_op jit(solution)/shard_map/psum | solution.py:86
  1389.1 1.4 fusion.66
  1390.5 88.8 %all-gather.2 = f32[128,256]{1,0:T(8,128)S(1)} all-gather(f32[32,256]{1,0:T(8,128)S(1)} %get-tuple-element.108), channel_id=4, replica_groups=mesh['rep'=4,'shard'=32,'tp'=4] {'rep'}, dimensions={0}, use_global_device_ids=true | all-gather | bytes 163840 | tf_op jit(solution)/shard_map/all_gather | solution.py:119
  1479.3 1.6 fusion.22
  1480.9 1.4 convolution_multiply_fusion
  1483.0 12.2 all-gather.1
  1497.0 11.9 all-gather
  1510.4 40.2 %while.11 = (s32[]{:T(128)}, f32[250,256]{1,0:T(8,128)S(1)}, s32[32,512]{1,0:T(8,128)S(1)}, s32[]{:T(128)}, bf16[32,512,256]{2,1,0:T(8,128)(2,1)}, /*index=5*/s32[]{:T(128)}, s32[]{:T(128)}) while((s32[]{:T(128)}, f32[250,256]{1,0:T(8,128)S(1)}, s32[32,512]{1,0:T(8,128)S(1)}, s32[]{:T(128)}, bf16[32,512,256]{2,1,0:T(8,128)(2,1)}, ...), condition=%wide.region_22.26_spmd.clone, body=%wide.region_21.25_spmd.clone.sunk | while | flops 65792512 | bytes 780895 | solution.py:37
  1510.4 1.2 convolution_add_fusion.2
  1511.6 1.2 convolution_add_fusion.2
  1512.9 1.2 convolution_add_fusion.2
  1514.2 1.2 convolution_add_fusion.2
  1515.4 1.2 convolution_add_fusion.2
  1516.7 1.2 convolution_add_fusion.2
  1517.9 1.2 convolution_add_fusion.2
  1519.2 1.2 convolution_add_fusion.2
  1520.4 1.2 convolution_add_fusion.2
  1521.7 1.2 convolution_add_fusion.2
  1523.0 1.2 convolution_add_fusion.2
  1524.2 1.2 convolution_add_fusion.2
  1525.5 1.2 convolution_add_fusion.2
  1526.7 1.2 convolution_add_fusion.2
  1528.0 1.2 convolution_add_fusion.2
  1529.2 1.2 convolution_add_fusion.2
  1530.5 1.2 convolution_add_fusion.2
  1531.8 1.2 convolution_add_fusion.2
  1533.0 1.2 convolution_add_fusion.2
  1534.3 1.2 convolution_add_fusion.2
  1535.5 1.2 convolution_add_fusion.2
  1536.8 1.2 convolution_add_fusion.2
  1538.0 1.2 convolution_add_fusion.2
  1539.3 1.2 convolution_add_fusion.2
  1540.6 1.2 convolution_add_fusion.2
  1543.1 1.2 convolution_add_fusion.2
  1544.3 1.2 convolution_add_fusion.2
  1548.1 1.2 convolution_add_fusion.2
  1549.4 1.2 convolution_add_fusion.2
  1550.7 13.8 all-gather.4
  (130 shorter events, 33.9 us)
Async XLA Ops:
  7.2 1.0 copy-start
  7.2 1502.4 %copy-start.2 = (bf16[1,32,2048]{2,1,0:T(8,128)(2,1)S(1)}, bf16[1,32,2048]{2,1,0:T(8,128)(2,1)}, u32[]{:S(2)}) copy-start(bf16[1,32,2048]{2,1,0:T(8,128)(2,1)} %param.34) | copy-start | bytes 393220
  7.2 1502.4 %copy-start.1 = (f32[1,32,2048]{2,1,0:T(8,128)S(1)}, f32[1,32,2048]{2,1,0:T(8,128)}, u32[]{:S(2)}) copy-start(f32[1,32,2048]{2,1,0:T(8,128)} %param.35) | copy-start | bytes 786436
  7.2 1501.7 %copy-start.4 = (bf16[1,32,768]{2,1,0:T(8,128)(2,1)S(1)}, bf16[1,32,768]{2,1,0:T(8,128)(2,1)}, u32[]{:S(2)}) copy-start(bf16[1,32,768]{2,1,0:T(8,128)(2,1)} %param.29) | copy-start | bytes 147460
  7.2 1501.7 %copy-start.3 = (f32[1,32,768]{2,1,0:T(8,128)S(1)}, f32[1,32,768]{2,1,0:T(8,128)}, u32[]{:S(2)}) copy-start(f32[1,32,768]{2,1,0:T(8,128)} %param.30) | copy-start | bytes 294916
  7.2 1475.0 %copy-start.8 = (f32[1,1,8,2048]{3,2,1,0:T(8,128)S(1)}, f32[1,1,8,2048]{3,2,1,0:T(8,128)}, u32[]{:S(2)}) copy-start(f32[1,1,8,2048]{3,2,1,0:T(8,128)} %param.37) | copy-start | bytes 196612
  7.3 1475.0 %copy-start.7 = (f32[1,1,8,2048]{3,2,1,0:T(8,128)S(1)}, f32[1,1,8,2048]{3,2,1,0:T(8,128)}, u32[]{:S(2)}) copy-start(f32[1,1,8,2048]{3,2,1,0:T(8,128)} %param.38) | copy-start | bytes 196612
  7.3 1489.1 %copy-start.10 = (f32[1,1,8,768]{3,2,1,0:T(8,128)S(1)}, f32[1,1,8,768]{3,2,1,0:T(8,128)}, u32[]{:S(2)}) copy-start(f32[1,1,8,768]{3,2,1,0:T(8,128)} %param.32) | copy-start | bytes 73732
  7.3 1489.1 %copy-start.9 = (f32[1,1,8,768]{3,2,1,0:T(8,128)S(1)}, f32[1,1,8,768]{3,2,1,0:T(8,128)}, u32[]{:S(2)}) copy-start(f32[1,1,8,768]{3,2,1,0:T(8,128)} %param.33) | copy-start | bytes 73732
  7.3 1543.3 %copy-start.6 = (f32[1,1,250,256]{3,1,2,0:T(1,128)S(1)}, f32[1,1,250,256]{3,1,2,0:T(1,128)}, u32[]{:S(2)}) copy-start(f32[1,1,250,256]{3,1,2,0:T(1,128)} %param.49) | copy-start | bytes 768004
  7.3 1543.3 %copy-start.5 = (f32[1,1,250,256]{3,1,2,0:T(1,128)S(1)}, f32[1,1,250,256]{3,1,2,0:T(1,128)}, u32[]{:S(2)}) copy-start(f32[1,1,250,256]{3,1,2,0:T(1,128)} %param.50) | copy-start | bytes 768004
  7.3 610.4 %all-reduce.11.cloned.1.call-start = ((), (), s32[]{:S(2)}) async-start(), calls=%async_computation.2 | async-start | bytes 720896 | tf_op jit(solution)/shard_map/psum | solution.py:86
  189.5 1291.4 %all-reduce.9.cloned.1.call-start = ((), (), s32[]{:S(2)}) async-start(), calls=%async_computation.1 | async-start | bytes 720896 | tf_op jit(solution)/shard_map/psum | solution.py:86
  870.5 639.9 %all-gather.7.cloned.1.call-start = ((), (), s32[]{:S(2)}) async-start(), calls=%async_computation | async-start | bytes 8454144 | tf_op jit(solution)/shard_map/all_gather | solution.py:109
Sparse Core Ops, SparseCore 0:
  189.7 336.8 all-reduce.10
  870.6 329.9 all-reduce.8
  1203.8 142.4 all-gather.6
where the time goes:
time: 1580 us
  blocking collectives  1440 us (91%)
  matrix products  61.4 us (4%)
  other arithmetic  49 us (3%)
    psum x2, blocking collectives, on_device(): lax.psum((raw_rights[0], raw_rights[1], raw_rights[2]), ('rep', 'shard'))  834 us
    psum x2, blocking collectives, on_device(): lefts = [lax.psum(left_part, ('rep', 'tp')) for left_part in parts]  204 us
    psum x2, blocking collectives, on_device(): summed = lax.psum((grams[0], grams[1], grams[2]), 'shard')  187 us
    all_gather x1, blocking collectives, on_device(): lax.all_gather(flats_new[2], 'rep', axis=1, tiled=True)  88.8 us
    all_gather x1, blocking collectives, on_device(): lax.all_gather(emb_ids, ('rep', 'shard'), axis=1, tiled=True)  82 us
    dot_general x32, matrix products, one_block(): jnp.dot(one_hot, block_values, preferred_element_type=jnp.float32)  38.6 us
  transfers between devices with their start and end apart: 3, of which 0 were waited for; matrix products, arithmetic and copies ran while one was open for 2% of the time, Pallas kernels for 0%

commit v1 on v0

--- a/solution.py
+++ b/solution.py
@@ -6,6 +6,11 @@
 ROUNDS = 2
 momentum_decay = 0.9
 step_size = 0.05
+
+
+def all_by_exchange(shard, mesh_axis, dim):
+    stack = jnp.stack([shard] * lax.axis_size(mesh_axis))
+    return jnp.concatenate(lax.all_to_all(stack, mesh_axis, 0, 0), axis=dim)
 
 
 def solve_right(lower_factor, values):
@@ -105,7 +110,7 @@
     row_start = (shard_index * rep_count + rep_index) * block_rows
     initial = jnp.zeros((block_rows, row_width), jnp.float32)
     pieces = (
-        lax.all_gather(emb_ids, ("rep", "shard"), axis=1, tiled=True),
+        all_by_exchange(emb_ids, ("rep", "shard"), 1),
         lax.all_gather(emb_grad, ("rep", "shard"), axis=1, tiled=True),
     )
     row_ids = pieces[0].reshape(-1)

time: 1580 us -> 1510 us (0.956)
  blocking collectives: 1440 us -> 1360 us
  starting transfers between devices: 0.12 us -> 18.3 us
    all_gather x1 -> x0, blocking collectives: 82 us -> none  [on_device(): lax.all_gather(emb_ids, ('rep', 'shard'), axis=1, tiled=True)]
    all_to_all x0 -> x1, starting transfers between devices: none -> 18.2 us  [all_by_exchange(): return jnp.concatenate(lax.all_to_all(stack, mesh_axis, 0, 0), axis=dim)]
  transfers between devices with their start and end apart: 3 -> 4, of which waited for: 0 -> 0; matrix products, arithmetic and copies ran while one was open for 2% -> 2% of each run, Pallas kernels for 0% -> 0%
where the time goes in v1:
time: 1510 us
  blocking collectives  1360 us (90%)
  matrix products  61.4 us (4%)
  other arithmetic  49 us (3%)
  starting transfers between devices  18.3 us (1%)
    psum x2, blocking collectives, on_device(): lax.psum((raw_rights[0], raw_rights[1], raw_rights[2]), ('rep', 'shard'))  834 us
    psum x2, blocking collectives, on_device(): lefts = [lax.psum(left_part, ('rep', 'tp')) for left_part in parts]  204 us
    psum x2, blocking collectives, on_device(): summed = lax.psum((grams[0], grams[1], grams[2]), 'shard')  187 us
    all_gather x1, blocking collectives, on_device(): lax.all_gather(flats_new[2], 'rep', axis=1, tiled=True)  88.9 us
    dot_general x32, matrix products, one_block(): jnp.dot(one_hot, block_values, preferred_element_type=jnp.float32)  38.6 us
  transfers between devices with their start and end apart: 4, of which 0 were waited for; matrix products, arithmetic and copies ran while one was open for 2% of the time, Pallas kernels for 0%

profile of v1, /device:TPU:16, one launch (start us, length us, event | category | flops | bytes accessed | tf_op | source)
XLA Modules:
  0.0 1512.4 jit_solution(6474778436480141727)
XLA Ops:
  8.1 1.3 fusion.11
  9.4 1.2 fusion.20
  11.9 62.7 %all-reduce.5 = (f32[32,32]{1,0:T(8,128)S(1)}, f32[32,32]{1,0:T(8,128)S(1)}, f32[128,32]{0,1:T(8,128)S(1)}) all-reduce(f32[32,32]{1,0:T(8,128)S(1)} %fusion.29, f32[32,32]{1,0:T(8,128)S(1)} %fusion.11, f32[128,32]{0,1:T(8,128)S(1)} %fusion.20), channel_id=1, replica_groups=mesh['rep'=4,'shard'=32,'tp'=4] {'rep','tp'}, use_global_device_ids=true, to_apply=%region_0.0 | all-reduce | flops 6144 | bytes 49152 | tf_op jit(solution)/shard_map/psum | solution.py:83
  75.1 96.4 %all-reduce.3 = (f32[32,32]{0,1:T(8,128)S(1)}, f32[32,32]{0,1:T(8,128)S(1)}, f32[32,32]{0,1:T(8,128)S(1)}) all-reduce(f32[32,32]{0,1:T(8,128)S(1)} %fusion.68, f32[32,32]{0,1:T(8,128)S(1)} %fusion.70, f32[32,32]{0,1:T(8,128)S(1)} %fusion.72), channel_id=1, replica_groups=mesh['rep'=4,'shard'=32,'tp'=4] {'shard'}, use_global_device_ids=true, to_apply=%region_1.0 | all-reduce | flops 3072 | bytes 24576 | tf_op jit(solution)/shard_map/psum | solution.py:85
  171.7 2.9 cholesky.126
  176.0 2.4 custom-call.15
  178.7 2.1 fusion.9
  180.8 2.9 cholesky.104
  185.1 2.4 custom-call.13
  187.7 1.8 fusion.27
  189.6 2.9 cholesky.148
  193.8 2.4 custom-call.17
  197.6 418.9 %psum.147 = f32[256,32]{0,1:T(8,128)S(1)} all-reduce(f32[256,32]{0,1:T(8,128)S(1)} %fusion.18), channel_id=1, replica_groups=mesh['rep'=4,'shard'=32,'tp'=4] {'rep','shard'}, use_global_device_ids=true, to_apply=%region_16.0 | all-reduce | flops 8192 | bytes 65536 | tf_op jit(solution)/shard_map/psum | solution.py:91
  618.9 1.4 fusion.7
  620.3 141.7 %all-reduce.4 = (f32[32,32]{1,0:T(8,128)S(1)}, f32[32,32]{1,0:T(8,128)S(1)}, f32[128,32]{0,1:T(8,128)S(1)}) all-reduce(f32[32,32]{1,0:T(8,128)S(1)} %fusion.25, f32[32,32]{1,0:T(8,128)S(1)} %fusion.7, f32[128,32]{0,1:T(8,128)S(1)} %fusion.16), channel_id=1, replica_groups=mesh['rep'=4,'shard'=32,'tp'=4] {'rep','tp'}, use_global_device_ids=true, to_apply=%region_5.8 | all-reduce | flops 6144 | bytes 49152 | tf_op jit(solution)/shard_map/psum | solution.py:83
  762.6 90.1 %all-reduce.2 = (f32[32,32]{0,1:T(8,128)S(1)}, f32[32,32]{0,1:T(8,128)S(1)}, f32[32,32]{0,1:T(8,128)S(1)}) all-reduce(f32[32,32]{0,1:T(8,128)S(1)} %fusion.69, f32[32,32]{0,1:T(8,128)S(1)} %fusion.71, f32[32,32]{0,1:T(8,128)S(1)} %fusion.73), channel_id=1, replica_groups=mesh['rep'=4,'shard'=32,'tp'=4] {'shard'}, use_global_device_ids=true, to_apply=%region_6.9 | all-reduce | flops 3072 | bytes 24576 | tf_op jit(solution)/shard_map/psum | solution.py:85
  852.7 2.9 cholesky.137
  857.0 2.4 custom-call.16
  859.6 2.1 fusion.5
  861.8 2.9 cholesky.115
  866.0 2.4 custom-call.14
  868.7 1.8 fusion.23
  871.2 1.3 stack.2
  872.6 18.2 %all-to-all-start = ((s32[128,1,128]{2,1,0:T(1,128)}), s32[128,1,128]{2,1,0:T(1,128)S(1)}, u32[]{:S(2)}, u32[]{:S(2)}) async-start(s32[128,1,128]{2,1,0:T(1,128)} %stack.2), calls=%async_computation | async-start | bytes 131072 | tf_op jit(solution)/shard_map/all_to_all | solution.py:13
  891.4 8.5 psum.151
  901.2 2.9 cholesky.159
  905.5 2.4 custom-call.18
  909.2 415.4 %psum.150 = f32[256,32]{0,1:T(8,128)S(1)} all-reduce(f32[256,32]{0,1:T(8,128)S(1)} %fusion.14), channel_id=1, replica_groups=mesh['rep'=4,'shard'=32,'tp'=4] {'rep','shard'}, use_global_device_ids=true, to_apply=%region_19.23 | all-reduce | flops 8192 | bytes 65536 | tf_op jit(solution)/shard_map/psum | solution.py:91
  1325.0 1.4 fusion.66
  1326.4 88.9 %all-gather.2 = f32[128,256]{1,0:T(8,128)S(1)} all-gather(f32[32,256]{1,0:T(8,128)S(1)} %get-tuple-element.108), channel_id=4, replica_groups=mesh['rep'=4,'shard'=32,'tp'=4] {'rep'}, dimensions={0}, use_global_device_ids=true | all-gather | bytes 163840 | tf_op jit(solution)/shard_map/all_gather | solution.py:124
  1415.3 1.6 fusion.22
  1418.2 1.4 convolution_multiply_fusion
  1420.3 12.2 all-gather.1
  1434.4 11.9 all-gather
  1447.7 40.2 %while.11 = (s32[]{:T(128)}, f32[250,256]{1,0:T(8,128)S(1)}, s32[32,512]{1,0:T(8,128)S(1)}, s32[]{:T(128)}, bf16[32,512,256]{2,1,0:T(8,128)(2,1)}, /*index=5*/s32[]{:T(128)}, s32[]{:T(128)}) while((s32[]{:T(128)}, f32[250,256]{1,0:T(8,128)S(1)}, s32[32,512]{1,0:T(8,128)S(1)}, s32[]{:T(128)}, bf16[32,512,256]{2,1,0:T(8,128)(2,1)}, ...), condition=%wide.region_22.26_spmd.clone, body=%wide.region_21.25_spmd.clone.sunk | while | flops 65792512 | bytes 780895 | solution.py:42
  1450.2 1.2 convolution_add_fusion.2
  1451.5 1.2 convolution_add_fusion.2
  1455.3 1.2 convolution_add_fusion.2
  1456.5 1.2 convolution_add_fusion.2
  1457.8 1.2 convolution_add_fusion.2
  1459.0 1.2 convolution_add_fusion.2
  1460.3 1.2 convolution_add_fusion.2
  1461.5 1.2 convolution_add_fusion.2
  1462.8 1.2 convolution_add_fusion.2
  1464.1 1.2 convolution_add_fusion.2
  1465.3 1.2 convolution_add_fusion.2
  1466.6 1.2 convolution_add_fusion.2
  1467.8 1.2 convolution_add_fusion.2
  1469.1 1.2 convolution_add_fusion.2
  1470.3 1.2 convolution_add_fusion.2
  1471.6 1.2 convolution_add_fusion.2
  1472.9 1.2 convolution_add_fusion.2
  1474.1 1.2 convolution_add_fusion.2
  1475.4 1.2 convolution_add_fusion.2
  1476.6 1.2 convolution_add_fusion.2
  1477.9 1.2 convolution_add_fusion.2
  1479.1 1.2 convolution_add_fusion.2
  1480.4 1.2 convolution_add_fusion.2
  1481.7 1.2 convolution_add_fusion.2
  1482.9 1.2 convolution_add_fusion.2
  1484.2 1.2 convolution_add_fusion.2
  1485.4 1.2 convolution_add_fusion.2
  1486.7 1.2 convolution_add_fusion.2
  1488.0 13.8 all-gather.4
  (132 shorter events, 35.1 us)
Async XLA Ops:
  7.2 1.0 copy-start
  7.2 1439.8 %copy-start.2 = (bf16[1,32,2048]{2,1,0:T(8,128)(2,1)S(1)}, bf16[1,32,2048]{2,1,0:T(8,128)(2,1)}, u32[]{:S(2)}) copy-start(bf16[1,32,2048]{2,1,0:T(8,128)(2,1)} %param.34) | copy-start | bytes 393220
  7.2 1439.7 %copy-start.1 = (f32[1,32,2048]{2,1,0:T(8,128)S(1)}, f32[1,32,2048]{2,1,0:T(8,128)}, u32[]{:S(2)}) copy-start(f32[1,32,2048]{2,1,0:T(8,128)} %param.35) | copy-start | bytes 786436
  7.2 1439.1 %copy-start.4 = (bf16[1,32,768]{2,1,0:T(8,128)(2,1)S(1)}, bf16[1,32,768]{2,1,0:T(8,128)(2,1)}, u32[]{:S(2)}) copy-start(bf16[1,32,768]{2,1,0:T(8,128)(2,1)} %param.29) | copy-start | bytes 147460
  7.2 1439.1 %copy-start.3 = (f32[1,32,768]{2,1,0:T(8,128)S(1)}, f32[1,32,768]{2,1,0:T(8,128)}, u32[]{:S(2)}) copy-start(f32[1,32,768]{2,1,0:T(8,128)} %param.30) | copy-start | bytes 294916
  7.2 1412.4 %copy-start.8 = (f32[1,1,8,2048]{3,2,1,0:T(8,128)S(1)}, f32[1,1,8,2048]{3,2,1,0:T(8,128)}, u32[]{:S(2)}) copy-start(f32[1,1,8,2048]{3,2,1,0:T(8,128)} %param.37) | copy-start | bytes 196612
  7.3 1412.4 %copy-start.7 = (f32[1,1,8,2048]{3,2,1,0:T(8,128)S(1)}, f32[1,1,8,2048]{3,2,1,0:T(8,128)}, u32[]{:S(2)}) copy-start(f32[1,1,8,2048]{3,2,1,0:T(8,128)} %param.38) | copy-start | bytes 196612
  7.3 1426.5 %copy-start.10 = (f32[1,1,8,768]{3,2,1,0:T(8,128)S(1)}, f32[1,1,8,768]{3,2,1,0:T(8,128)}, u32[]{:S(2)}) copy-start(f32[1,1,8,768]{3,2,1,0:T(8,128)} %param.32) | copy-start | bytes 73732
  7.3 1426.5 %copy-start.9 = (f32[1,1,8,768]{3,2,1,0:T(8,128)S(1)}, f32[1,1,8,768]{3,2,1,0:T(8,128)}, u32[]{:S(2)}) copy-start(f32[1,1,8,768]{3,2,1,0:T(8,128)} %param.33) | copy-start | bytes 73732
  7.3 1480.6 %copy-start.6 = (f32[1,1,250,256]{3,1,2,0:T(1,128)S(1)}, f32[1,1,250,256]{3,1,2,0:T(1,128)}, u32[]{:S(2)}) copy-start(f32[1,1,250,256]{3,1,2,0:T(1,128)} %param.49) | copy-start | bytes 768004
  7.3 1480.6 %copy-start.5 = (f32[1,1,250,256]{3,1,2,0:T(1,128)S(1)}, f32[1,1,250,256]{3,1,2,0:T(1,128)}, u32[]{:S(2)}) copy-start(f32[1,1,250,256]{3,1,2,0:T(1,128)} %param.50) | copy-start | bytes 768004
  7.3 610.4 %all-reduce.11.cloned.1.call-start = ((), (), s32[]{:S(2)}) async-start(), calls=%async_computation.3 | async-start | bytes 720896 | tf_op jit(solution)/shard_map/psum | solution.py:91
  189.5 1228.7 %all-reduce.9.cloned.1.call-start = ((), (), s32[]{:S(2)}) async-start(), calls=%async_computation.2 | async-start | bytes 720896 | tf_op jit(solution)/shard_map/psum | solution.py:91
  870.5 577.2 %all-gather.7.cloned.1.call-start = ((), (), s32[]{:S(2)}) async-start(), calls=%async_computation.1 | async-start | bytes 8454144 | tf_op jit(solution)/shard_map/all_gather | solution.py:114
  872.6 544.3 %all-to-all-start = ((s32[128,1,128]{2,1,0:T(1,128)}), s32[128,1,128]{2,1,0:T(1,128)S(1)}, u32[]{:S(2)}, u32[]{:S(2)}) async-start(s32[128,1,128]{2,1,0:T(1,128)} %stack.2), calls=%async_computation | async-start | bytes 131072 | tf_op jit(solution)/shard_map/all_to_all | solution.py:13
Sparse Core Ops, SparseCore 0:
  189.7 336.8 all-reduce.10
  870.6 330.4 all-reduce.8
  1204.2 142.0 all-gather.6
